TPU v7x, 32 devices: a whole 2x2x4 slice. The times are simulated.
32 devices in a mesh: dp: 8 (over z, x), tensor: 4 (over y, core).
Axes of the slice: x: 2, y: 2, z: 4, core: 2. Of those that a mesh axis runs over, the one named last changes fastest.
Arguments:
- tokens: bfloat16 [32768, 768], P(('dp', 'tensor')), may hold values from -6 to 6
- cotangent: bfloat16 [32768, 768], P(('dp', 'tensor')), may hold values from -26 to 26
- seq_group: int32 [16], P('dp'), may hold values from 0 to 1
- block_slot: int32 [13830], replicated, may hold values from 0 to 20751, as said below
- master: float32 [4, 20752, 128], P('tensor', 'dp'), may hold values from -3 to 3
- first_moment: float32 [4, 20752, 128], P('tensor', 'dp'), may hold values from -1 to 1
- second_moment: float32 [4, 20752, 128], P('tensor', 'dp'), may hold values from 0 to 1, as said below
Outputs:
- output: bfloat16 [32768, 768], P(('dp', 'tensor'))
- input_grad: float32 [32768, 768], P(('dp', 'tensor'))
- group_norms: float32 [16], P('dp')
- new_master: float32 [4, 20752, 128], P('tensor', 'dp')
- new_first: float32 [4, 20752, 128], P('tensor', 'dp')
- new_second: float32 [4, 20752, 128], P('tensor', 'dp')
Inputs may be any that keep to these rules, and one draw needn't show every extreme that they name: `block_slot`: all entries differ; slot s belongs to the owner with dp index s // 2594; one owner holds 2594 blocks. `seq_group`: group ids count within one dp index: sequences of different dp indices never share a group. `second_moment`: Positive.
All inputs are finite; a program needn't handle non-finite values.
Results may differ from a plain program's by a relative error of at most 0.012.
Values may be sent and summed in bfloat16 or wider, within the bound.
No kernel may reach another device: no remote copies, remote signals or barrier semaphores. Data moves between devices by JAX's collectives and lax.ppermute only.
A program may use at most 256 MiB of HBM per device.

v0:
```python
import jax
import jax.numpy as jnp
from jax import lax
from jax.sharding import PartitionSpec as P

HEADS = 12
HD = 64
ROT = 16
FF = 3072
eps_norm = 1e-05
eps_adam = 1e-08
beta_one = 0.5
beta_two = 0.6
root_half = 0.7071067811865476
inv_root_tau = 0.3989422804014327


def rotary_tables(length, rot_dims):
    half_rot = rot_dims // 2
    frequency = 10000.0 ** (-2.0 * jnp.arange(half_rot, dtype=jnp.float32) / rot_dims)
    angles = jnp.arange(length, dtype=jnp.float32)[:, None] * frequency[None, :]
    return (jnp.cos(angles), jnp.sin(angles))


def rotate(features, cosine, sine_table, rot_dims):
    half_rot = rot_dims // 2
    first_half = features[..., :half_rot]
    second_half = features[..., half_rot:rot_dims]
    cos_cols = cosine[:, None, :]
    sin_cols = sine_table[:, None, :]
    return jnp.concatenate(
        [
            first_half * cos_cols - second_half * sin_cols,
            second_half * cos_cols + first_half * sin_cols,
            features[..., rot_dims:],
        ],
        axis=-1,
    )


def unrotate(grad_in, cosine, sine_table, rot_dims):
    half_rot = rot_dims // 2
    first_half = grad_in[..., :half_rot]
    second_half = grad_in[..., half_rot:rot_dims]
    cos_cols = cosine[:, None, :]
    sin_cols = sine_table[:, None, :]
    return jnp.concatenate(
        [
            first_half * cos_cols + second_half * sin_cols,
            second_half * cos_cols - first_half * sin_cols,
            grad_in[..., rot_dims:],
        ],
        axis=-1,
    )


def layer_norm(rows_in):
    row_mean = jnp.mean(rows_in, axis=-1, keepdims=True)
    centred = rows_in - row_mean
    inverse = lax.rsqrt(jnp.mean(centred * centred, axis=-1, keepdims=True) + eps_norm)
    return (centred * inverse, inverse)


def unpack(flat_params, d_model, heads_local, ff_local, width_local):
    inner_width = heads_local * HD
    end_qkv = d_model * 3 * inner_width
    end_out = end_qkv + inner_width * d_model
    end_up = end_out + d_model * ff_local
    end_down = end_up + ff_local * d_model
    return (
        flat_params[:end_qkv].reshape(d_model, 3 * inner_width),
        flat_params[end_qkv:end_out].reshape(inner_width, d_model),
        flat_params[end_out:end_up].reshape(d_model, ff_local),
        flat_params[end_up:end_down].reshape(ff_local, d_model),
        flat_params[end_down:].reshape(4, width_local),
    )


def step_rates(position, d_model, heads_local, head_dim, ff_local, seq_len, ff_all):
    end_qkv = d_model * 3 * heads_local * head_dim
    end_out = end_qkv + heads_local * head_dim * d_model
    end_up = end_out + d_model * ff_local
    end_down = end_up + ff_local * d_model
    matrix_rate = d_model ** (-0.5)
    learn_rate = jnp.where(
        position < end_qkv,
        matrix_rate,
        jnp.where(
            position < end_out,
            (seq_len / (5.0 * d_model)) ** 0.5,
            jnp.where(
                position < end_up,
                matrix_rate,
                jnp.where(position < end_down, ff_all ** (-0.5), 0.1),
            ),
        ),
    )
    weight_decay = jnp.where(position < end_down, 0.1, 0.0)
    return (learn_rate.astype(jnp.float32), weight_decay.astype(jnp.float32))


def adam_update(weight, moment_one, moment_two, gradient, learn_rate, weight_decay):
    new_one = beta_one * moment_one + (1.0 - beta_one) * gradient
    new_two = beta_two * moment_two + (1.0 - beta_two) * gradient * gradient
    new_weight = weight - learn_rate * (
        new_one / (jnp.sqrt(new_two) + eps_adam) + weight_decay * weight
    )
    return (new_weight, new_one, new_two)


def by_sequence(tensor_in, seq_count):
    return tensor_in.reshape(seq_count, -1, tensor_in.shape[-1])


def seq_product(left, right, seq_count):
    return jnp.einsum(
        "sli,slj->sij",
        by_sequence(left, seq_count),
        by_sequence(right, seq_count),
        preferred_element_type=jnp.float32,
    )


def on_device(tokens, cotangent, seq_group, block_slot, master, first_moment, second_moment):
    tensor_count = lax.axis_size("tensor")
    tensor_rank = lax.axis_index("tensor")
    owner_index = lax.axis_index("dp")
    owner_count = lax.axis_size("dp")
    d_model = tokens.shape[1]
    local_rows = tokens.shape[0]
    width_local = d_model // tensor_count
    heads_local = HEADS // tensor_count
    inner_width = heads_local * HD
    ff_local = FF // tensor_count
    seq_count = seq_group.shape[0]
    tok_count = local_rows * tensor_count
    seq_len = tok_count // seq_count
    capacity = master.shape[1]
    block_width = master.shape[2]
    block_count = block_slot.shape[0]
    copies = lax.all_gather(master[0].astype(jnp.bfloat16), "dp", axis=0, tiled=True)
    flat_params = copies[block_slot].reshape(-1)
    w_qkv, w_out, w_up, w_down, norm_local = unpack(
        flat_params, d_model, heads_local, ff_local, width_local
    )
    x_full, norm_rows = (
        lax.all_gather(tokens, "tensor", axis=0, tiled=True),
        lax.all_gather(norm_local.reshape(1, 4 * width_local), "tensor", axis=0, tiled=True),
    )
    norm_full = jnp.transpose(norm_rows.reshape(tensor_count, 4, width_local), (1, 0, 2)).reshape(
        4, d_model
    )
    rows_full = x_full.astype(jnp.float32)
    normed, inverse = layer_norm(rows_full)
    norm_gains = norm_full.astype(jnp.float32)
    first_in = (normed * norm_gains[0] + norm_gains[1]).astype(jnp.bfloat16)
    second_in = (normed * norm_gains[2] + norm_gains[3]).astype(jnp.bfloat16)
    projected = jnp.dot(first_in, w_qkv, preferred_element_type=jnp.float32).reshape(
        seq_count, seq_len, 3, heads_local, HD
    )
    cosine, sine_table = rotary_tables(seq_len, ROT)
    queries = rotate(projected[:, :, 0], cosine, sine_table, ROT).astype(jnp.bfloat16)
    key_rows = rotate(projected[:, :, 1], cosine, sine_table, ROT).astype(jnp.bfloat16)
    values = projected[:, :, 2].astype(jnp.bfloat16)
    block_rows = min(512, seq_len)
    block_total = seq_len // block_rows
    scale_factor = HD ** (-0.5)
    starts = jnp.arange(block_total, dtype=jnp.int32) * block_rows
    key_index = jnp.arange(seq_len, dtype=jnp.int32)

    def scores_of(row_start):
        query_block = lax.dynamic_slice_in_dim(queries, row_start, block_rows, 1)
        scores = (
            jnp.einsum("sqhd,skhd->shqk", query_block, key_rows, preferred_element_type=jnp.float32)
            * scale_factor
        )
        allowed = (row_start + jnp.arange(block_rows, dtype=jnp.int32))[:, None] >= key_index[
            None, :
        ]
        return (jnp.where(allowed, scores, -1e30), query_block)

    def forward_block(row_start):
        scores = scores_of(row_start)[0]
        row_peak = jnp.max(scores, axis=-1, keepdims=True)
        exp_scores = jnp.exp(scores - row_peak)
        row_total = jnp.sum(exp_scores, axis=-1, keepdims=True)
        weights_low = (exp_scores / row_total).astype(jnp.bfloat16)
        mixed_heads = jnp.einsum(
            "shqk,skhd->sqhd", weights_low, values, preferred_element_type=jnp.float32
        )
        return (mixed_heads, row_peak + jnp.log(row_total))

    mixed_heads, log_sums = lax.map(forward_block, starts)
    attended = jnp.moveaxis(mixed_heads, 0, 1).reshape(tok_count, inner_width).astype(jnp.bfloat16)
    hidden_pre = jnp.dot(second_in, w_up, preferred_element_type=jnp.float32)
    hidden_low = jax.nn.gelu(hidden_pre, approximate=False).astype(jnp.bfloat16)
    branch = jnp.dot(attended, w_out, preferred_element_type=jnp.float32) + jnp.dot(
        hidden_low, w_down, preferred_element_type=jnp.float32
    )
    branch_sum = lax.psum_scatter(
        branch.astype(jnp.bfloat16), "tensor", scatter_dimension=0, tiled=True
    ).astype(jnp.float32)
    output = (tokens.astype(jnp.float32) + branch_sum).astype(jnp.bfloat16)
    back_full = lax.all_gather(cotangent, "tensor", axis=0, tiled=True)
    grad_down = seq_product(hidden_low, back_full, seq_count)
    grad_hidden = jnp.dot(back_full, w_down.T, preferred_element_type=jnp.float32)
    cumulative = 0.5 * (1.0 + lax.erf(hidden_pre * root_half))
    density = jnp.exp(-0.5 * hidden_pre * hidden_pre) * inv_root_tau
    grad_pre = (grad_hidden * (cumulative + hidden_pre * density)).astype(jnp.bfloat16)
    grad_up = seq_product(second_in, grad_pre, seq_count)
    second_back = jnp.dot(grad_pre, w_up.T, preferred_element_type=jnp.float32)
    grad_out = seq_product(attended, back_full, seq_count)
    grad_attended = jnp.dot(back_full, w_out.T, preferred_element_type=jnp.float32).astype(
        jnp.bfloat16
    )
    grad_blocks_in = jnp.moveaxis(
        grad_attended.reshape(seq_count, block_total, block_rows, heads_local, HD), 1, 0
    )

    def backward_block(carried, inputs):
        row_start, log_sum, grad_block = inputs
        scores, query_block = scores_of(row_start)
        probs = jnp.exp(scores - log_sum)
        grad_probs = jnp.einsum(
            "sqhd,skhd->shqk", grad_block, values, preferred_element_type=jnp.float32
        )
        row_dot = jnp.sum(probs * grad_probs, axis=-1, keepdims=True)
        grad_scores = (probs * (grad_probs - row_dot)).astype(jnp.bfloat16)
        grad_query = (
            jnp.einsum("shqk,skhd->sqhd", grad_scores, key_rows, preferred_element_type=jnp.float32)
            * scale_factor
        )
        grad_keys = (
            carried[0]
            + jnp.einsum(
                "shqk,sqhd->skhd", grad_scores, query_block, preferred_element_type=jnp.float32
            )
            * scale_factor
        )
        grad_values = carried[1] + jnp.einsum(
            "shqk,sqhd->skhd",
            probs.astype(jnp.bfloat16),
            grad_block,
            preferred_element_type=jnp.float32,
        )
        return ((grad_keys, grad_values), grad_query)

    zero_heads = jnp.zeros((seq_count, seq_len, heads_local, HD), jnp.float32)
    key_value_grads, grad_queries = lax.scan(
        backward_block, (zero_heads, zero_heads), (starts, log_sums, grad_blocks_in)
    )
    grad_queries = jnp.moveaxis(grad_queries, 0, 1).reshape(seq_count, seq_len, heads_local, HD)
    grad_qkv = (
        jnp.stack(
            [
                unrotate(grad_queries, cosine, sine_table, ROT),
                unrotate(key_value_grads[0], cosine, sine_table, ROT),
                key_value_grads[1],
            ],
            axis=2,
        )
        .reshape(tok_count, 3 * inner_width)
        .astype(jnp.bfloat16)
    )
    grad_qkv_w = seq_product(first_in, grad_qkv, seq_count)
    first_back = jnp.dot(grad_qkv, w_qkv.T, preferred_element_type=jnp.float32)
    row_start_local = tensor_rank * local_rows
    first_sum, second_sum = (
        lax.psum_scatter(
            first_back.astype(jnp.bfloat16), "tensor", scatter_dimension=0, tiled=True
        ).astype(jnp.float32),
        lax.psum_scatter(
            second_back.astype(jnp.bfloat16), "tensor", scatter_dimension=0, tiled=True
        ).astype(jnp.float32),
    )
    normed_rows = lax.dynamic_slice_in_dim(normed, row_start_local, local_rows, 0)
    inverse_rows = lax.dynamic_slice_in_dim(inverse, row_start_local, local_rows, 0)
    scaled_first = first_sum * norm_gains[0]
    scaled_second = second_sum * norm_gains[2]
    first_mean = jnp.mean(scaled_first, axis=1, keepdims=True)
    first_cross = jnp.mean(scaled_first * normed_rows, axis=1, keepdims=True)
    second_mean = jnp.mean(scaled_second, axis=1, keepdims=True)
    second_cross = jnp.mean(scaled_second * normed_rows, axis=1, keepdims=True)
    grad_input = (
        cotangent.astype(jnp.float32)
        + inverse_rows * (scaled_first - first_mean - normed_rows * first_cross)
        + inverse_rows * (scaled_second - second_mean - normed_rows * second_cross)
    )
    row_seq = (row_start_local + jnp.arange(local_rows, dtype=jnp.int32)) // seq_len
    row_member = (row_seq[None, :] == jnp.arange(seq_count, dtype=jnp.int32)[:, None]).astype(
        jnp.float32
    )
    partial_sums = jnp.stack(
        [
            jnp.dot(row_member, first_sum * normed_rows, precision=lax.Precision.HIGHEST),
            jnp.dot(row_member, first_sum, precision=lax.Precision.HIGHEST),
            jnp.dot(row_member, second_sum * normed_rows, precision=lax.Precision.HIGHEST),
            jnp.dot(row_member, second_sum, precision=lax.Precision.HIGHEST),
        ],
        axis=1,
    )
    norm_grads = lax.psum_scatter(partial_sums, "tensor", scatter_dimension=2, tiled=True)
    per_seq = jnp.concatenate(
        [
            grad_qkv_w.reshape(seq_count, -1),
            grad_out.reshape(seq_count, -1),
            grad_up.reshape(seq_count, -1),
            grad_down.reshape(seq_count, -1),
            norm_grads.reshape(seq_count, -1),
        ],
        axis=1,
    )
    member = (seq_group[None, :] == jnp.arange(seq_count, dtype=jnp.int32)[:, None]).astype(
        jnp.float32
    )
    group_grads = jnp.dot(member, per_seq, precision=lax.Precision.HIGHEST)
    squares = lax.psum(jnp.sum(group_grads * group_grads, axis=1), "tensor")
    group_norms = jnp.sqrt(squares)
    clip_scale = 1.0 / jnp.maximum(group_norms, 1.0)
    clipped = jnp.dot(clip_scale, group_grads, precision=lax.Precision.HIGHEST)
    grad_rows = clipped.reshape(block_count, block_width)
    slot_total = owner_count * capacity
    slot_block = (
        jnp.full((slot_total,), -1, jnp.int32)
        .at[block_slot]
        .set(jnp.arange(block_count, dtype=jnp.int32))
    )
    my_blocks = lax.dynamic_slice_in_dim(slot_block, owner_index * capacity, capacity)
    summed = lax.psum(grad_rows, "dp")
    owned_grad = jnp.where(my_blocks[:, None] >= 0, summed[jnp.maximum(my_blocks, 0)], 0.0)
    position = (
        jnp.maximum(my_blocks, 0)[:, None] * block_width
        + jnp.arange(block_width, dtype=jnp.int32)[None, :]
    )
    learn_rate, weight_decay = step_rates(position, d_model, heads_local, HD, ff_local, seq_len, FF)
    new_weight, new_one, new_two = adam_update(
        master[0], first_moment[0], second_moment[0], owned_grad, learn_rate, weight_decay
    )
    return (output, grad_input, group_norms, new_weight[None], new_one[None], new_two[None])


def solution(mesh):
    placed = (
        P(("dp", "tensor"), None),
        P(("dp", "tensor"), None),
        P("dp"),
        P(),
        P("tensor", "dp", None),
        P("tensor", "dp", None),
        P("tensor", "dp", None),
    )
    return jax.shard_map(
        on_device,
        mesh=mesh,
        in_specs=placed,
        out_specs=(
            P(("dp", "tensor"), None),
            P(("dp", "tensor"), None),
            P("dp"),
            P("tensor", "dp", None),
            P("tensor", "dp", None),
            P("tensor", "dp", None),
        ),
        check_vma=False,
    )
```

profile of v0, /device:TPU:0, one launch (start us, length us, event | category | flops | bytes accessed | tf_op | source)
XLA Modules:
  0.0 1451.3 jit_solution(10674566761597092681)
XLA Ops:
  17.1 148.8 %all-gather.10.cloned.1.call-done = bf16[1,20752,128]{2,0,1:T(2,128)(2,1)} async-done(((bf16[1,2594,128]{2,0,1:T(2,128)(2,1)}), bf16[1,20752,128]{2,0,1:T(2,128)(2,1)}) %all-gather.10.cloned.1.call-update) | async-done | bytes 5312528 | tf_op jit(solution)/shard_map/all_gather | solution.py:141
  174.4 30.7 %gather_fusion = bf16[13830,128]{1,0:T(8,128)(2,1)S(1)} fusion(bf16[20752,128]{1,0:T(8,128)(2,1)} %bitcast.203, s32[14336]{0:T(1024)} %pad_clamp_fusion), kind=kCustom, calls=%fused_computation | custom fusion | bytes 7136280 | tf_op jit(solution)/shard_map/gather | solution.py:142
  276.1 163.2 %while.30 = (s32[]{:T(128)}, bf16[4,2,512,3,64]{2,4,3,1,0:T(8,128)(2,1)}, f32[4,2,3,512,1]{3,2,1,4,0:T(4,128)S(1)}, s32[4]{0:T(128)S(1)}, bf16[2,2048,3,64]{1,3,...) while((s32[]{:T(128)}, ...), condition=%wide.region_5.6_spmd.clone.clone, body=%wide.region_2.5_spmd.clone.sunk.clone | while | flops 1687156224 | bytes 96723152 | solution.py:193
  280.0 12.1 fusion.178
  292.1 12.1 fusion.179
  320.8 12.1 fusion.178
  332.9 12.1 fusion.179
  361.6 12.1 fusion.178
  373.7 12.1 fusion.179
  385.8 11.6 fusion.180
  402.4 12.1 fusion.178
  414.5 12.1 fusion.179
  439.3 336.2 %while.31 = (s32[]{:T(128)}, f32[2,2048,3,64]{1,3,2,0:T(8,128)}, f32[2,2048,3,64]{1,3,2,0:T(8,128)}, f32[4,2,512,3,64]{2,4,3,1,0:T(8,128)}, s32[4]{0:T(128)S(1)}...) while((s32[]{:T(128)}, f32[2,2048,3,64]{1,3,2,0:T(8,128)}, ...), condition=%wide.region_9.10_spmd.clone.clone, body=%wide.region_7.9_spmd.clone.sunk.clone | while | flops 4126078464 | bytes 275603712 | solution.py:249
  454.8 12.9 bitcast_add_fusion.7
  467.7 18.1 %multiply_reduce_fusion.4 = (f32[2,3,512]{2,1,0:T(4,128)S(1)}, f32[2,3,512,2048]{3,2,1,0:T(8,128)}) fusion(f32[2,3,512,2048]{3,2,1,0:T(8,128)} %fusion.190, f32[2,3,512]{2,1,0:T(4,128)S(1)} %dynamic-slice_bitcast_fusion.3, pred[512,2048]{1,0:T(8,128)(4,1)S(1)} %iota_compare_fusion.12, bf16[2,2048,3,64]{1,3,2,0:T(8,128)(2,1)} %copy-done.1, ...), kind=kOutput, calls=%fused_computation.22.clone.1.clone | convolution fusion | flops 836760576 | bytes 53370884 | tf_op jit(solution)/shard_map/while/body/eval_jaxpr/sqhd,skhd->shqk/dot_general | solution.py:224
  485.8 17.0 %multiply_convert_fusion.3 = bf16[2,3,512,2048]{3,2,1,0:T(8,128)(2,1)S(1)} fusion(f32[2,3,512,2048]{3,2,1,0:T(8,128)} %get-tuple-element.409, f32[2,3,512,2048]{3,2,1,0:T(8,128)} %fusion.190, f32[2,3,512]{2,1,0:T(4,128)S(1)} %get-tuple-element.410, f32[2,3,512]{2,1,0:T(4,128)S(1)} %dynamic-slice_bitcast_fusion.3, ...), kind=kLoop, calls=%fused_computation.21.clone.1.clone | loop fusion | flops 37748736 | bytes 63987712 | tf_op jit(solution)/shard_map/while/body/eval_jaxpr/convert_element_type | solution.py:228
  537.3 13.8 bitcast_add_fusion.7
  551.1 18.1 %multiply_reduce_fusion.4 = (f32[2,3,512]{2,1,0:T(4,128)S(1)}, f32[2,3,512,2048]{3,2,1,0:T(8,128)}) fusion(f32[2,3,512,2048]{3,2,1,0:T(8,128)} %fusion.190, f32[2,3,512]{2,1,0:T(4,128)S(1)} %dynamic-slice_bitcast_fusion.3, pred[512,2048]{1,0:T(8,128)(4,1)S(1)} %iota_compare_fusion.12, bf16[2,2048,3,64]{1,3,2,0:T(8,128)(2,1)} %copy-done.1, ...), kind=kOutput, calls=%fused_computation.22.clone.1.clone | convolution fusion | flops 836760576 | bytes 53370884 | tf_op jit(solution)/shard_map/while/body/eval_jaxpr/sqhd,skhd->shqk/dot_general | solution.py:224
  569.2 17.0 %multiply_convert_fusion.3 = bf16[2,3,512,2048]{3,2,1,0:T(8,128)(2,1)S(1)} fusion(f32[2,3,512,2048]{3,2,1,0:T(8,128)} %get-tuple-element.409, f32[2,3,512,2048]{3,2,1,0:T(8,128)} %fusion.190, f32[2,3,512]{2,1,0:T(4,128)S(1)} %get-tuple-element.410, f32[2,3,512]{2,1,0:T(4,128)S(1)} %dynamic-slice_bitcast_fusion.3, ...), kind=kLoop, calls=%fused_computation.21.clone.1.clone | loop fusion | flops 37748736 | bytes 63987712 | tf_op jit(solution)/shard_map/while/body/eval_jaxpr/convert_element_type | solution.py:228
  621.7 13.8 bitcast_add_fusion.7
  635.5 18.1 %multiply_reduce_fusion.4 = (f32[2,3,512]{2,1,0:T(4,128)S(1)}, f32[2,3,512,2048]{3,2,1,0:T(8,128)}) fusion(f32[2,3,512,2048]{3,2,1,0:T(8,128)} %fusion.190, f32[2,3,512]{2,1,0:T(4,128)S(1)} %dynamic-slice_bitcast_fusion.3, pred[512,2048]{1,0:T(8,128)(4,1)S(1)} %iota_compare_fusion.12, bf16[2,2048,3,64]{1,3,2,0:T(8,128)(2,1)} %copy-done.1, ...), kind=kOutput, calls=%fused_computation.22.clone.1.clone | convolution fusion | flops 836760576 | bytes 53370884 | tf_op jit(solution)/shard_map/while/body/eval_jaxpr/sqhd,skhd->shqk/dot_general | solution.py:224
  653.6 17.0 %multiply_convert_fusion.3 = bf16[2,3,512,2048]{3,2,1,0:T(8,128)(2,1)S(1)} fusion(f32[2,3,512,2048]{3,2,1,0:T(8,128)} %get-tuple-element.409, f32[2,3,512,2048]{3,2,1,0:T(8,128)} %fusion.190, f32[2,3,512]{2,1,0:T(4,128)S(1)} %get-tuple-element.410, f32[2,3,512]{2,1,0:T(4,128)S(1)} %dynamic-slice_bitcast_fusion.3, ...), kind=kLoop, calls=%fused_computation.21.clone.1.clone | loop fusion | flops 37748736 | bytes 63987712 | tf_op jit(solution)/shard_map/while/body/eval_jaxpr/convert_element_type | solution.py:228
  706.1 13.8 bitcast_add_fusion.7
  719.9 18.1 %multiply_reduce_fusion.4 = (f32[2,3,512]{2,1,0:T(4,128)S(1)}, f32[2,3,512,2048]{3,2,1,0:T(8,128)}) fusion(f32[2,3,512,2048]{3,2,1,0:T(8,128)} %fusion.190, f32[2,3,512]{2,1,0:T(4,128)S(1)} %dynamic-slice_bitcast_fusion.3, pred[512,2048]{1,0:T(8,128)(4,1)S(1)} %iota_compare_fusion.12, bf16[2,2048,3,64]{1,3,2,0:T(8,128)(2,1)} %copy-done.1, ...), kind=kOutput, calls=%fused_computation.22.clone.1.clone | convolution fusion | flops 836760576 | bytes 53370884 | tf_op jit(solution)/shard_map/while/body/eval_jaxpr/sqhd,skhd->shqk/dot_general | solution.py:224
  738.0 17.0 %multiply_convert_fusion.3 = bf16[2,3,512,2048]{3,2,1,0:T(8,128)(2,1)S(1)} fusion(f32[2,3,512,2048]{3,2,1,0:T(8,128)} %get-tuple-element.409, f32[2,3,512,2048]{3,2,1,0:T(8,128)} %fusion.190, f32[2,3,512]{2,1,0:T(4,128)S(1)} %get-tuple-element.410, f32[2,3,512]{2,1,0:T(4,128)S(1)} %dynamic-slice_bitcast_fusion.3, ...), kind=kLoop, calls=%fused_computation.21.clone.1.clone | loop fusion | flops 37748736 | bytes 63987712 | tf_op jit(solution)/shard_map/while/body/eval_jaxpr/convert_element_type | solution.py:228
  840.7 33.3 %fusion.41 = (bf16[4096,768]{1,0:T(8,128)(2,1)}, f32[4096,768]{1,0:T(8,128)S(1)}) fusion(bf16[4096,768]{1,0:T(8,128)(2,1)} %get-tuple-element.243, bf16[768,768]{1,0:T(8,128)(2,1)S(1)} %copy-done.22), kind=kOutput, calls=%fused_computation.59 | convolution fusion | flops 5036310528 | bytes 26345472 | tf_op jit(solution)/shard_map/dot_general | solution.py:195
  917.7 12.2 convolution_bitcast_fusion
  946.8 21.3 %reduce-scatter.11.cloned.1.call-done = bf16[1024,768]{1,0:T(8,128)(2,1)} async-done(((bf16[4096,768]{1,0:T(8,128)(2,1)}), bf16[1024,768]{1,0:T(8,128)(2,1)}) %reduce-scatter.11.cloned.1.call-update) | async-done | bytes 1572880 | tf_op jit(solution)/shard_map/reduce_scatter | solution.py:272
  1002.3 41.5 %multiply_reduce_fusion.1 = (f32[2]{0:T(128)S(1)}, f32[2,1770240]{1,0:T(2,128)}) fusion(f32[2,1770240]{1,0:T(2,128)} %constant_dynamic-update-slice_fusion, s32[2]{0:T(128)S(1)} %copy-done.37), kind=kOutput, calls=%fused_computation.55 | convolution fusion | flops 92052480 | bytes 28323856 | tf_op jit(solution)/shard_map/dot_general | solution.py:316
  1050.1 119.3 %convolution_reduce_fusion = f32[1770240]{0:T(1024)} fusion(f32[2,1770240]{1,0:T(2,128)} %get-tuple-element.263, f32[2]{0:T(128)S(1)} %sqrt.7), kind=kOutput, calls=%fused_computation.116 | convolution fusion | flops 42485764 | bytes 21242888 | tf_op jit(solution)/shard_map/dot_general | solution.py:320
  1169.4 65.6 %scatter_custom_fusion = s32[20752]{0:T(1024)S(1)} fusion(s32[13830]{0:T(1024)} %copy-done.27, s32[13830]{0:T(1024)S(1)} %iota.92, s32[]{:T(128)} %constant.72.clone.1), kind=kCustom, calls=%fused_computation.158 | custom fusion | bytes 83520 | tf_op jit(solution)/shard_map/scatter | solution.py:326
  1246.7 157.5 %all-reduce.2.cloned.1.call-done = f32[13830,128]{1,0:T(8,128)} async-done(((f32[13830,128]{1,0:T(8,128)}), f32[13830,128]{1,0:T(8,128)}) %all-reduce.2.cloned.1.call-update) | async-done | bytes 7080976 | tf_op jit(solution)/shard_map/psum | solution.py:329
  (302 shorter events, 486.2 us)
Async XLA Ops:
  7.2 158.7 %all-gather.10.cloned.1.call-start = ((), (), s32[]{:S(2)}) async-start(), calls=%async_computation.10 | async-start | bytes 11953152 | tf_op jit(solution)/shard_map/all_gather | solution.py:141
  10.8 217.5 %all-gather.6.cloned.1.call-start = ((), (), s32[]{:S(2)}) async-start(), calls=%async_computation.4 | async-start | bytes 7864320 | tf_op jit(solution)/shard_map/all_gather | solution.py:147
  11.6 248.4 %all-gather.8.cloned.1.call-start = ((), (), s32[]{:S(2)}) async-start(), calls=%async_computation.6 | async-start | bytes 7864320 | tf_op jit(solution)/shard_map/all_gather | solution.py:204
  12.3 929.1 %reduce-scatter.9.cloned.1.call-start = ((), (), s32[]{:S(2)}) async-start(), calls=%async_computation.7 | async-start | bytes 7864320 | tf_op jit(solution)/shard_map/reduce_scatter | solution.py:269
  214.3 20.6 %copy-start.31 = (f32[768]{0:T(1024)}, f32[768]{0:T(1024)S(1)}, u32[]{:S(2)}) copy-start(f32[768]{0:T(1024)S(1)} %mul.459) | copy-start | bytes 9220
  214.4 20.5 %copy-start.33 = (f32[768]{0:T(1024)}, f32[768]{0:T(1024)S(1)}, u32[]{:S(2)}) copy-start(f32[768]{0:T(1024)S(1)} %mul.475) | copy-start | bytes 9220
  246.9 13.1 copy-start.18
  292.1 12.1 copy-start.7
  332.9 12.1 copy-start.7
  373.7 12.1 copy-start.7
  414.5 12.1 copy-start.7
  512.5 9.5 copy-start.2
  596.9 9.5 copy-start.2
  681.3 9.5 copy-start.2
  765.7 9.5 copy-start.2
  788.4 9.5 copy-start.9
  799.1 9.3 slice-start
  838.3 129.8 %reduce-scatter.11.cloned.1.call-start = ((), (), s32[]{:S(2)}) async-start(), calls=%async_computation.8 | async-start | bytes 7864320 | tf_op jit(solution)/shard_map/reduce_scatter | solution.py:272
  838.3 35.7 %slice-start.2 = ((s8[6291456]{0:T(1024)(128)(4,1)}), s8[4194304]{0:T(1024)(128)(4,1)S(1)}, s32[]{:S(2)}) async-start(s8[6291456]{0:T(1024)(128)(4,1)} %bitcast.218), calls=%async_computation.14 | async-start | bytes 8388608
  840.6 33.3 %slice-start.3 = ((s8[6291456]{0:T(1024)(128)(4,1)}), s8[2097152]{0:T(1024)(128)(4,1)S(1)}, s32[]{:S(2)}) async-start(s8[6291456]{0:T(1024)(128)(4,1)} %bitcast.218), calls=%async_computation.15 | async-start | bytes 4194304
  840.7 33.3 %copy-start.20 = (bf16[768,768]{1,0:T(8,128)(2,1)S(1)}, bf16[768,768]{1,0:T(8,128)(2,1)}, u32[]{:S(2)}) copy-start(bf16[768,768]{1,0:T(8,128)(2,1)} %reshape.377) | copy-start | bytes 3538948
  909.1 91.2 %reduce-scatter.13.cloned.1.call-start = ((), (), s32[]{:S(2)}) async-start(), calls=%async_computation.11 | async-start | bytes 491520
  917.7 12.2 copy-start.21
  929.9 11.5 copy-start.28
  946.8 30.2 %copy-start.19 = (bf16[192,768]{1,0:T(8,128)(2,1)S(1)}, bf16[192,768]{1,0:T(8,128)(2,1)}, u32[]{:S(2)}) copy-start(bf16[192,768]{1,0:T(8,128)(2,1)} %reshape.375) | copy-start | bytes 884740
  976.5 262.1 %reduce-scatter.7.cloned.1.call-start = ((), (), s32[]{:S(2)}) async-start(), calls=%async_computation.5 | async-start | bytes 7864320 | tf_op jit(solution)/shard_map/reduce_scatter | solution.py:200
  994.2 410.0 %all-reduce.2.cloned.1.call-start = ((), (), s32[]{:S(2)}) async-start(), calls=%async_computation.9 | async-start | bytes 14163968 | tf_op jit(solution)/shard_map/psum | solution.py:329
  1050.1 119.3 %copy-start.40 = (f32[2]{0:T(128)}, f32[2]{0:T(128)S(1)}, u32[]{:S(2)}) copy-start(f32[2]{0:T(128)S(1)} %sqrt.7) | copy-start | bytes 28
  1169.4 65.9 %copy-start.5 = (bf16[1024,768]{1,0:T(8,128)(2,1)S(1)}, bf16[1024,768]{1,0:T(8,128)(2,1)}, u32[]{:S(2)}) copy-start(bf16[1024,768]{1,0:T(8,128)(2,1)} %reduce-scatter.9.cloned.1.call-done) | copy-start | bytes 4718596
  1169.4 65.9 %copy-start.32 = (f32[768]{0:T(1024)S(1)}, f32[768]{0:T(1024)}, u32[]{:S(2)}) copy-start(f32[768]{0:T(1024)} %copy-done.31) | copy-start | bytes 9220
  1169.4 65.9 %copy-start.34 = (f32[768]{0:T(1024)S(1)}, f32[768]{0:T(1024)}, u32[]{:S(2)}) copy-start(f32[768]{0:T(1024)} %copy-done.33) | copy-start | bytes 9220
  1246.7 165.3 %copy-start.14 = (f32[1,2594,128]{2,0,1:T(1,128)S(1)}, f32[1,2594,128]{2,0,1:T(1,128)}, u32[]{:S(2)}) copy-start(f32[1,2594,128]{2,0,1:T(1,128)} %param.15) | copy-start | bytes 3984388
  (39 other events, 161.8 us)
Sparse Core Ops, SparseCore 0:
  10.9 154.8 all-gather.9
  167.4 44.5 all-gather.5
  213.6 46.4 all-gather.7
  838.4 58.8 reduce-scatter.8
  909.2 58.8 reduce-scatter.10
  976.7 20.7 reduce-scatter.12
  1000.0 58.9 reduce-scatter.6
  1169.5 234.6 all-reduce.1
where the time goes:
time: 1460 us; the launch traced here: 1450 us
  matrix products  624 us (43%)
  waiting for transfers between devices  339 us (23%)
  local copies, waits for them, and re-layouts  273 us (19%)
  other arithmetic  172 us (12%)
  loops' own time  16.5 us (1%)
  between operations  15.2 us (1%)
    psum x1, waiting for transfers between devices, on_device(): summed = lax.psum(grad_rows, 'dp')  158 us
    all_gather x1, waiting for transfers between devices, on_device(): lax.all_gather(master[0].astype(jnp.bfloat16), 'dp', axis=0, tiled=True)  149 us
    dot_general x1, matrix products, on_device(): clipped = jnp.dot(clip_scale, group_grads, precision=lax.Precision.HIGHEST)  119 us
    dot_general x8, matrix products, scores_of(): jnp.einsum('sqhd,skhd->shqk', query_block, key_rows, preferred_element_ty...  93.7 us
    unnamed x100, local copies, waits for them, and re-layouts  83.8 us
    dot_general x4, matrix products, backward_block(): jnp.einsum('sqhd,skhd->shqk', grad_block, values, preferred_element_type=...  72.5 us
    convert_element_type x4, other arithmetic, backward_block(): grad_scores = (probs * (grad_probs - row_dot)).astype(jnp.bfloat16)  68.2 us
    scatter x1, local copies, waits for them, and re-layouts, on_device(): slot_block = jnp.full((slot_total,), -1, jnp.int32).at[block_slot].set(jn...  65.6 us
  transfers between devices with their start and end apart: 8, of which 4 were waited for; matrix products, arithmetic and copies ran while one was open for 31% of the time, Pallas kernels for 0%

commit v1 on v0

--- a/solution.py
+++ b/solution.py
@@ -326,7 +326,7 @@
         .set(jnp.arange(block_count, dtype=jnp.int32))
     )
     my_blocks = lax.dynamic_slice_in_dim(slot_block, owner_index * capacity, capacity)
-    summed = lax.psum(grad_rows, "dp")
+    summed = jnp.sum(lax.all_gather(grad_rows, "dp"), axis=0)
     owned_grad = jnp.where(my_blocks[:, None] >= 0, summed[jnp.maximum(my_blocks, 0)], 0.0)
     position = (
         jnp.maximum(my_blocks, 0)[:, None] * block_width

time: 1460 us -> 2320 us (1.59)
  waiting for transfers between devices: 339 us -> 1180 us
    all_gather x0 -> x1, waiting for transfers between devices: none -> 995 us  [on_device(): summed = jnp.sum(lax.all_gather(grad_rows, 'dp'), axis=0)]
    psum x1 -> x0, waiting for transfers between devices: 158 us -> none  [on_device(): summed = lax.psum(grad_rows, 'dp')]
  transfers between devices with their start and end apart: 8 -> 8, of which waited for: 4 -> 4; matrix products, arithmetic and copies ran while one was open for 31% -> 20% of each run, Pallas kernels for 0% -> 0%
where the time goes in v1:
time: 2320 us; the launch traced here: 2310 us
  waiting for transfers between devices  1180 us (51%)
  matrix products  625 us (27%)
  local copies, waits for them, and re-layouts  273 us (12%)
  other arithmetic  192 us (8%)
    all_gather x1, waiting for transfers between devices, on_device(): summed = jnp.sum(lax.all_gather(grad_rows, 'dp'), axis=0)  995 us
    all_gather x1, waiting for transfers between devices, on_device(): lax.all_gather(master[0].astype(jnp.bfloat16), 'dp', axis=0, tiled=True)  149 us
    dot_general x1, matrix products, on_device(): clipped = jnp.dot(clip_scale, group_grads, precision=lax.Precision.HIGHEST)  119 us
    dot_general x8, matrix products, scores_of(): jnp.einsum('sqhd,skhd->shqk', query_block, key_rows, preferred_element_ty...  93.7 us
    unnamed x100, local copies, waits for them, and re-layouts  83.8 us
    dot_general x4, matrix products, backward_block(): jnp.einsum('sqhd,skhd->shqk', grad_block, values, preferred_element_type=...  72.5 us
    convert_element_type x4, other arithmetic, backward_block(): grad_scores = (probs * (grad_probs - row_dot)).astype(jnp.bfloat16)  68.2 us
    scatter x1, local copies, waits for them, and re-layouts, on_device(): slot_block = jnp.full((slot_total,), -1, jnp.int32).at[block_slot].set(jn...  65.6 us
  transfers between devices with their start and end apart: 8, of which 4 were waited for; matrix products, arithmetic and copies ran while one was open for 20% of the time, Pallas kernels for 0%

profile of v1, /device:TPU:0, one launch (start us, length us, event | category | flops | bytes accessed | tf_op | source)
XLA Modules:
  0.0 2310.0 jit_solution(8579699420731872991)
XLA Ops:
  17.0 148.9 %all-gather.13.cloned.1.call-done = bf16[1,20752,128]{2,0,1:T(2,128)(2,1)} async-done(((bf16[1,2594,128]{2,0,1:T(2,128)(2,1)}), bf16[1,20752,128]{2,0,1:T(2,128)(2,1)}) %all-gather.13.cloned.1.call-update) | async-done | bytes 5312528 | tf_op jit(solution)/shard_map/all_gather | solution.py:141
  174.4 30.7 %gather_fusion = bf16[13830,128]{1,0:T(8,128)(2,1)S(1)} fusion(bf16[20752,128]{1,0:T(8,128)(2,1)} %bitcast.203, s32[14336]{0:T(1024)} %pad_clamp_fusion), kind=kCustom, calls=%fused_computation | custom fusion | bytes 7136280 | tf_op jit(solution)/shard_map/gather | solution.py:142
  276.1 163.2 %while.30 = (s32[]{:T(128)}, bf16[4,2,512,3,64]{2,4,3,1,0:T(8,128)(2,1)}, f32[4,2,3,512,1]{3,2,1,4,0:T(4,128)S(1)}, s32[4]{0:T(128)S(1)}, bf16[2,2048,3,64]{1,3,...) while((s32[]{:T(128)}, ...), condition=%wide.region_5.6_spmd.clone.clone, body=%wide.region_2.5_spmd.clone.sunk.clone | while | flops 1687156224 | bytes 96723152 | solution.py:193
  280.0 12.1 fusion.178
  292.1 12.1 fusion.179
  320.8 12.1 fusion.178
  332.9 12.1 fusion.179
  361.6 12.1 fusion.178
  373.7 12.1 fusion.179
  402.4 12.1 fusion.178
  414.5 12.1 fusion.179
  439.3 336.4 %while.31 = (s32[]{:T(128)}, f32[2,2048,3,64]{1,3,2,0:T(8,128)}, f32[2,2048,3,64]{1,3,2,0:T(8,128)}, f32[4,2,512,3,64]{2,4,3,1,0:T(8,128)}, s32[4]{0:T(128)S(1)}...) while((s32[]{:T(128)}, f32[2,2048,3,64]{1,3,2,0:T(8,128)}, ...), condition=%wide.region_9.10_spmd.clone.clone, body=%wide.region_7.9_spmd.clone.sunk.clone | while | flops 4126078464 | bytes 275603712 | solution.py:249
  454.8 13.0 bitcast_add_fusion.7
  467.8 18.1 multiply_reduce_fusion.4
  485.9 17.0 multiply_convert_fusion.3
  537.4 13.8 bitcast_add_fusion.7
  551.2 18.1 multiply_reduce_fusion.4
  569.3 17.0 multiply_convert_fusion.3
  621.8 13.8 bitcast_add_fusion.7
  635.7 18.1 multiply_reduce_fusion.4
  653.8 17.0 multiply_convert_fusion.3
  706.2 13.8 bitcast_add_fusion.7
  720.1 18.1 multiply_reduce_fusion.4
  738.2 17.0 multiply_convert_fusion.3
  840.8 33.4 %fusion.41 = (bf16[4096,768]{1,0:T(8,128)(2,1)}, f32[4096,768]{1,0:T(8,128)S(1)}) fusion(bf16[4096,768]{1,0:T(8,128)(2,1)} %get-tuple-element.243, bf16[768,768]{1,0:T(8,128)(2,1)S(1)} %copy-done.22), kind=kOutput, calls=%fused_computation.59 | convolution fusion | flops 5036310528 | bytes 26345472 | tf_op jit(solution)/shard_map/dot_general | solution.py:195
  917.9 12.2 convolution_bitcast_fusion
  946.9 21.3 reduce-scatter.11.cloned.1.call-done
  1002.6 41.5 %multiply_reduce_fusion.1 = (f32[2]{0:T(128)S(1)}, f32[2,1770240]{1,0:T(2,128)}) fusion(f32[2,1770240]{1,0:T(2,128)} %constant_dynamic-update-slice_fusion, s32[2]{0:T(128)S(1)} %copy-done.37), kind=kOutput, calls=%fused_computation.55 | convolution fusion | flops 92052480 | bytes 28323856 | tf_op jit(solution)/shard_map/dot_general | solution.py:316
  1050.4 119.4 %convolution_reduce_fusion = f32[1770240]{0:T(1024)} fusion(f32[2,1770240]{1,0:T(2,128)} %get-tuple-element.263, f32[2]{0:T(128)S(1)} %sqrt.7), kind=kOutput, calls=%fused_computation.116 | convolution fusion | flops 42485764 | bytes 21242888 | tf_op jit(solution)/shard_map/dot_general | solution.py:320
  1169.8 65.6 %scatter_custom_fusion = s32[20752]{0:T(1024)S(1)} fusion(s32[13830]{0:T(1024)} %copy-done.27, s32[13830]{0:T(1024)S(1)} %iota.92, s32[]{:T(128)} %constant.72.clone.1), kind=kCustom, calls=%fused_computation.158 | custom fusion | bytes 83520 | tf_op jit(solution)/shard_map/scatter | solution.py:326
  1246.8 994.9 %all-gather.11.cloned.1.call-done = f32[8,13830,128]{2,1,0:T(8,128)} async-done(((f32[1,13830,128]{2,1,0:T(8,128)}), f32[8,13830,128]{2,1,0:T(8,128)}) %all-gather.11.cloned.1.call-update) | async-done | bytes 56647696 | tf_op jit(solution)/shard_map/all_gather | solution.py:329
  2241.7 21.1 reduce_sum.97
  (303 shorter events, 497.7 us)
Async XLA Ops:
  7.2 158.7 %all-gather.13.cloned.1.call-start = ((), (), s32[]{:S(2)}) async-start(), calls=%async_computation.10 | async-start | bytes 11953152 | tf_op jit(solution)/shard_map/all_gather | solution.py:141
  10.8 217.5 %all-gather.7.cloned.1.call-start = ((), (), s32[]{:S(2)}) async-start(), calls=%async_computation.4 | async-start | bytes 7864320 | tf_op jit(solution)/shard_map/all_gather | solution.py:147
  11.6 248.4 %all-gather.9.cloned.1.call-start = ((), (), s32[]{:S(2)}) async-start(), calls=%async_computation.6 | async-start | bytes 7864320 | tf_op jit(solution)/shard_map/all_gather | solution.py:204
  12.3 929.2 %reduce-scatter.9.cloned.1.call-start = ((), (), s32[]{:S(2)}) async-start(), calls=%async_computation.7 | async-start | bytes 7864320 | tf_op jit(solution)/shard_map/reduce_scatter | solution.py:269
  214.3 20.6 copy-start.31
  214.4 20.6 copy-start.33
  247.0 13.0 copy-start.18
  292.1 12.1 copy-start.7
  332.9 12.1 copy-start.7
  373.7 12.1 copy-start.7
  414.5 12.1 copy-start.7
  512.5 9.5 copy-start.2
  597.0 9.6 copy-start.2
  681.5 9.5 copy-start.2
  765.8 9.5 copy-start.2
  788.5 9.5 copy-start.9
  799.2 9.3 slice-start
  838.4 129.8 %reduce-scatter.11.cloned.1.call-start = ((), (), s32[]{:S(2)}) async-start(), calls=%async_computation.8 | async-start | bytes 7864320 | tf_op jit(solution)/shard_map/reduce_scatter | solution.py:272
  838.5 35.7 %slice-start.2 = ((s8[6291456]{0:T(1024)(128)(4,1)}), s8[4194304]{0:T(1024)(128)(4,1)S(1)}, s32[]{:S(2)}) async-start(s8[6291456]{0:T(1024)(128)(4,1)} %bitcast.218), calls=%async_computation.14 | async-start | bytes 8388608
  840.8 33.4 %slice-start.3 = ((s8[6291456]{0:T(1024)(128)(4,1)}), s8[2097152]{0:T(1024)(128)(4,1)S(1)}, s32[]{:S(2)}) async-start(s8[6291456]{0:T(1024)(128)(4,1)} %bitcast.218), calls=%async_computation.15 | async-start | bytes 4194304
  840.8 33.4 %copy-start.20 = (bf16[768,768]{1,0:T(8,128)(2,1)S(1)}, bf16[768,768]{1,0:T(8,128)(2,1)}, u32[]{:S(2)}) copy-start(bf16[768,768]{1,0:T(8,128)(2,1)} %reshape.374) | copy-start | bytes 3538948
  909.2 91.3 %reduce-scatter.13.cloned.1.call-start = ((), (), s32[]{:S(2)}) async-start(), calls=%async_computation.11 | async-start | bytes 491520
  917.9 12.2 copy-start.21
  930.1 11.5 copy-start.28
  946.9 30.2 %copy-start.19 = (bf16[192,768]{1,0:T(8,128)(2,1)S(1)}, bf16[192,768]{1,0:T(8,128)(2,1)}, u32[]{:S(2)}) copy-start(bf16[192,768]{1,0:T(8,128)(2,1)} %reshape.372) | copy-start | bytes 884740
  976.7 262.2 %reduce-scatter.7.cloned.1.call-start = ((), (), s32[]{:S(2)}) async-start(), calls=%async_computation.5 | async-start | bytes 7864320 | tf_op jit(solution)/shard_map/reduce_scatter | solution.py:200
  994.5 1247.2 %all-gather.11.cloned.1.call-start = ((), (), s32[]{:S(2)}) async-start(), calls=%async_computation.9 | async-start | bytes 63737856 | tf_op jit(solution)/shard_map/all_gather | solution.py:329
  994.5 8.0 copy-start.37
  1050.4 119.4 %copy-start.40 = (f32[2]{0:T(128)}, f32[2]{0:T(128)S(1)}, u32[]{:S(2)}) copy-start(f32[2]{0:T(128)S(1)} %sqrt.7) | copy-start | bytes 28
  1169.8 65.9 %copy-start.5 = (bf16[1024,768]{1,0:T(8,128)(2,1)S(1)}, bf16[1024,768]{1,0:T(8,128)(2,1)}, u32[]{:S(2)}) copy-start(bf16[1024,768]{1,0:T(8,128)(2,1)} %reduce-scatter.9.cloned.1.call-done) | copy-start | bytes 4718596
  1169.8 65.9 %copy-start.32 = (f32[768]{0:T(1024)S(1)}, f32[768]{0:T(1024)}, u32[]{:S(2)}) copy-start(f32[768]{0:T(1024)} %copy-done.31) | copy-start | bytes 9220
  1169.8 65.9 %copy-start.34 = (f32[768]{0:T(1024)S(1)}, f32[768]{0:T(1024)}, u32[]{:S(2)}) copy-start(f32[768]{0:T(1024)} %copy-done.33) | copy-start | bytes 9220
  (39 other events, 161.2 us)
Sparse Core Ops, SparseCore 0:
  10.9 154.8 all-gather.12
  167.4 44.5 all-gather.6
  213.6 46.4 all-gather.8
  838.5 58.8 reduce-scatter.8
  909.3 58.8 reduce-scatter.10
  976.8 20.7 reduce-scatter.12
  1000.2 58.9 reduce-scatter.6
  1169.9 1071.6 all-gather.10
